TPU v7x, 256 devices: a whole 4x4x8 slice. The times are simulated.
256 devices in a mesh: pipe: 8 (over y, x_lo), expert: 32 (over x_hi, z, core).
Axes of the slice: x: 4 (x_hi: 2, x_lo: 2; x = x_hi * 2 + x_lo), y: 4, z: 8, core: 2. Of those that a mesh axis runs over, the one named last changes fastest.
Arguments:
- tokens_in: bfloat16 [2, 2560, 2048], P(None, 'expert'), may hold values from -6 to 6
- out_grad: bfloat16 [2, 2560, 2048], P(None, 'expert'), may hold values from -6 to 6
- routes: int32 [8, 2, 2560, 1], P(None, None, 'expert'), may hold values from 0 to 31; in each aligned block of 80 rows (0 to 79, 80 to 159, ..., all dimensions but the last counted through in order) at most 3 rows name the same one
- router: bfloat16 [8, 2048, 32], P('pipe'), may hold values from -0.125 to 0.125
- norm_gain: bfloat16 [8, 2048], P('pipe'), may hold values from 0.5 to 1.5
- w_in: bfloat16 [8, 32, 2048, 1024], P('pipe', 'expert'), may hold values from -0.125 to 0.125
- w_out: bfloat16 [8, 32, 512, 2048], P('pipe', 'expert'), may hold values from -0.25 to 0.25
Outputs:
- grad_in: bfloat16 [8, 32, 2048, 1024], P('pipe', 'expert')
- grad_out: bfloat16 [8, 32, 512, 2048], P('pipe', 'expert')
Inputs may be any that keep to these rules, and one draw needn't show every extreme that they name: `routes`: in each aligned block of 80 rows (one device's tokens of one layer and microbatch) no expert is named by more than 3 tokens; a token's 1 ids differ.
All inputs are finite; a program needn't handle non-finite values.
Results may differ from a plain program's by a relative error of at most 0.029.
Values may be sent and summed in bfloat16 or wider, within the bound.
A program may use at most 128 MiB of HBM per device.

v0:
```python
import jax
import jax.numpy as jnp
from jax import lax
from jax.sharding import PartitionSpec as P

epsilon = 1e-06


def side_by_side(arrays, axis, split_dim, concat_dim, along):
    columns = [a.reshape(*a.shape[:along], -1) for a in arrays]
    both = jnp.concatenate(columns, axis=along)
    result, at, done = (
        lax.all_to_all(both, axis, split_axis=split_dim, concat_axis=concat_dim, tiled=True),
        0,
        [],
    )
    for a, column in zip(arrays, columns):
        share = result[..., at : at + column.shape[along]]
        done.append(share.reshape(*share.shape[:along], *a.shape[along:]))
        at += column.shape[along]
    return tuple(done)


def shifted(block, axis, distance):
    devices = range(lax.axis_size(axis))
    route = [(i - distance, i) for i in devices if i - distance in devices]
    return lax.ppermute(block, axis, route)


def normalize(hidden, gain_row):
    values = hidden.astype(jnp.float32)
    inverse = lax.rsqrt(jnp.mean(values * values, axis=-1, keepdims=True) + epsilon)
    scaled = values * inverse
    normed = (scaled * gain_row.astype(jnp.float32)).astype(jnp.bfloat16)
    return (normed, scaled, inverse)


def router_gates(normed, router_cols, route_ids):
    logits_all = jnp.dot(normed, router_cols, preferred_element_type=jnp.float32)
    picked = (
        route_ids[:, :, None] == jnp.arange(router_cols.shape[1], dtype=jnp.int32)[None, None, :]
    )
    logits = jnp.sum(jnp.where(picked, logits_all[:, None, :], 0.0), axis=-1)
    return (jax.nn.sigmoid(logits), picked)


def slot_positions(route_ids, expert_count, capacity):
    pair_ids = route_ids.reshape(-1)
    pair_marks = (pair_ids[:, None] == jnp.arange(expert_count, dtype=jnp.int32)[None, :]).astype(
        jnp.int32
    )
    earlier = jnp.cumsum(pair_marks, axis=0) - pair_marks
    return pair_ids * capacity + jnp.sum(earlier * pair_marks, axis=1)


def slot_owners(positions, slot_count):
    pair_count = positions.shape[0]
    owners = (
        jnp.zeros((slot_count,), jnp.int32)
        .at[positions]
        .set(jnp.arange(pair_count, dtype=jnp.int32))
    )
    filled = jnp.zeros((slot_count,), jnp.int32).at[positions].set(1)
    return (owners, filled > 0)


def to_slots(source, index_table, filled, slot_shape):
    gathered = source[index_table]
    mask_shape = (filled.shape[0],) + (1,) * (gathered.ndim - 1)
    chosen = jnp.where(filled.reshape(mask_shape), gathered, jnp.zeros((), source.dtype))
    return chosen.reshape(slot_shape)


def expert_forward(token_rows, weight_in, weight_out):
    inner_width = weight_out.shape[0]
    joined = jnp.dot(token_rows, weight_in, preferred_element_type=jnp.float32)
    gate_part = joined[:, :inner_width]
    activated = (gate_part * jax.nn.sigmoid(gate_part) * joined[:, inner_width:]).astype(
        jnp.bfloat16
    )
    return jnp.dot(activated, weight_out, preferred_element_type=jnp.float32).astype(jnp.bfloat16)


def expert_backward(token_rows, upstream, gate_share, weight_in, weight_out):
    inner_width = weight_out.shape[0]
    joined = jnp.dot(token_rows, weight_in, preferred_element_type=jnp.float32)
    gate_part = joined[:, :inner_width]
    up_part = joined[:, inner_width:]
    sigmoid_gate = jax.nn.sigmoid(gate_part)
    silu_gate = gate_part * sigmoid_gate
    activated = (silu_gate * up_part).astype(jnp.bfloat16)
    produced = jnp.dot(activated, weight_out, preferred_element_type=jnp.float32).astype(
        jnp.bfloat16
    )
    upstream_f = upstream.astype(jnp.float32)
    share_grad = jnp.sum(produced.astype(jnp.float32) * upstream_f, axis=-1)
    scaled_grad = (gate_share.astype(jnp.float32)[:, None] * upstream_f).astype(jnp.bfloat16)
    act_grad = jnp.dot(scaled_grad, weight_out.T, preferred_element_type=jnp.float32)
    gate_grad = act_grad * up_part * sigmoid_gate * (1.0 + gate_part * (1.0 - sigmoid_gate))
    up_grad = act_grad * silu_gate
    joined_grad = jnp.concatenate([gate_grad, up_grad], axis=-1).astype(jnp.bfloat16)
    rows_grad = jnp.dot(joined_grad, weight_in.T, preferred_element_type=jnp.float32).astype(
        jnp.bfloat16
    )
    return (rows_grad, share_grad, joined_grad, activated, scaled_grad)


def when_active(active, compute, operand):
    return lax.cond(
        active, compute, lambda values: jax.tree.map(jnp.zeros_like, compute(values)), operand
    )


def combine(hidden, gate_probs, pair_outputs):
    shares = lax.optimization_barrier(gate_probs.astype(jnp.bfloat16)).astype(jnp.float32)
    mixed = jnp.sum(shares[:, :, None] * pair_outputs.astype(jnp.float32), axis=1)
    return (hidden.astype(jnp.float32) + mixed).astype(jnp.bfloat16)


def token_backward(
    upstream, scaled, inverse, gain_row, router_cols, gate_probs, picked, pair_grads, pair_shares
):
    logit_grad = pair_shares.astype(jnp.float32) * gate_probs * (1.0 - gate_probs)
    spread = jnp.sum(jnp.where(picked, logit_grad[:, :, None], 0.0), axis=1)
    normed_grad = jnp.sum(pair_grads.astype(jnp.float32), axis=1) + jnp.dot(
        spread, router_cols.astype(jnp.float32).T
    )
    gained = normed_grad * gain_row.astype(jnp.float32)
    centred = gained - scaled * jnp.mean(gained * scaled, axis=-1, keepdims=True)
    return (upstream.astype(jnp.float32) + inverse * centred).astype(jnp.bfloat16)


def store_micro(stored, update, which_micro, in_range):
    current = lax.dynamic_index_in_dim(stored, which_micro, 0, keepdims=False)
    chosen = jnp.where(in_range, update, current)
    return lax.dynamic_update_index_in_dim(stored, chosen, which_micro, 0)


def weight_grads(rows, joined_grad, activated, scaled_grad):
    contract = (((0,), (0,)), ((), ()))
    grad_in = lax.dot_general(rows, joined_grad, contract, preferred_element_type=jnp.float32)
    grad_out = lax.dot_general(activated, scaled_grad, contract, preferred_element_type=jnp.float32)
    return (grad_in.astype(jnp.bfloat16)[None, None], grad_out.astype(jnp.bfloat16)[None, None])


def shards(tokens_in, out_grad, routes, router, norm_gain, w_in, w_out):
    sections = lax.axis_size("pipe")
    rank_count = lax.axis_size("expert")
    section_index = lax.axis_index("pipe")
    micro_count, tok_count, model_width = tokens_in.shape
    expert_count = router.shape[2]
    top_count = routes.shape[3]
    inner_width = w_out.shape[2]
    capacity = max(2, tok_count * top_count * 3 // (2 * expert_count))
    slot_count = expert_count * capacity
    slot_shape = (expert_count, capacity, model_width)
    row_count = rank_count * capacity
    own_in = w_in[0, 0]
    own_out = w_out[0, 0]
    own_router = router[0]
    own_gain = norm_gain[0]
    zero_value = jnp.zeros((), jnp.bfloat16)

    def prepare(hidden, gain_row, router_cols, route_ids):
        normed, scaled, inverse = normalize(hidden, gain_row)
        gate_probs, picked = router_gates(normed, router_cols, route_ids)
        positions = slot_positions(route_ids, expert_count, capacity)
        owners, filled = slot_owners(positions, slot_count)
        return (normed, scaled, inverse, gate_probs, picked, positions, owners, filled)

    def forward_layer(hidden, gain_row, router_cols, route_ids, run_forward):
        normed, scaled, inverse, gate_probs, picked, positions, owners, filled = prepare(
            hidden, gain_row, router_cols, route_ids
        )
        send_rows = to_slots(normed, owners // top_count, filled, slot_shape)
        received = lax.all_to_all(send_rows, "expert", split_axis=0, concat_axis=0, tiled=True)
        part_slots = received.shape[1]
        produced = run_forward(received.reshape(rank_count * part_slots, model_width))
        returned = lax.all_to_all(
            produced.reshape(rank_count, part_slots, model_width),
            "expert",
            split_axis=0,
            concat_axis=0,
            tiled=True,
        )
        returned, received = (returned, received)
        pair_outputs = returned.reshape(slot_count, model_width)[positions].reshape(
            tok_count, top_count, model_width
        )
        return (combine(hidden, gate_probs, pair_outputs), received)

    def backward_layer(hidden, upstream, gain_row, router_cols, route_ids, kept_rows, run_backward):
        normed, scaled, inverse, gate_probs, picked, positions, owners, filled = prepare(
            hidden, gain_row, router_cols, route_ids
        )
        send_grad = to_slots(upstream, owners // top_count, filled, slot_shape)
        send_share = to_slots(
            gate_probs.astype(jnp.bfloat16).reshape(-1), owners, filled, (expert_count, capacity)
        )
        got_grad, got_share = side_by_side((send_grad, send_share), "expert", 0, 0, 2)
        flat_rows = kept_rows.reshape(-1, model_width)
        rows_grad, share_grad, joined_grad, activated, scaled_grad = run_backward(
            flat_rows, got_grad.reshape(-1, model_width), got_share.reshape(-1)
        )
        back_rows, back_shares = side_by_side(
            (
                rows_grad.reshape(rank_count, capacity, model_width),
                share_grad.astype(jnp.bfloat16).reshape(rank_count, capacity),
            ),
            "expert",
            0,
            0,
            2,
        )
        pair_grads = back_rows.reshape(slot_count, model_width)[positions].reshape(
            tok_count, top_count, model_width
        )
        pair_shares = back_shares.reshape(slot_count)[positions].reshape(tok_count, top_count)
        passed = token_backward(
            upstream,
            scaled,
            inverse,
            gain_row,
            router_cols,
            gate_probs,
            picked,
            pair_grads,
            pair_shares,
        )
        return (passed, (flat_rows, joined_grad, activated, scaled_grad))

    kept_start = jnp.zeros((micro_count, rank_count, capacity, model_width), jnp.bfloat16)
    hidden_start = jnp.zeros((micro_count, tok_count, model_width), jnp.bfloat16)
    flat_zero = jnp.zeros((tok_count, model_width), jnp.bfloat16)
    records_start = (
        jnp.zeros((micro_count, row_count, model_width), jnp.bfloat16),
        jnp.zeros((micro_count, row_count, 2 * inner_width), jnp.bfloat16),
        jnp.zeros((micro_count, row_count, inner_width), jnp.bfloat16),
        jnp.zeros((micro_count, row_count, model_width), jnp.bfloat16),
    )
    layer_routes = lax.dynamic_index_in_dim(routes, section_index, 0, keepdims=False)
    total_steps = micro_count + sections - 1

    def forward_step(step_number, loop_state):
        incoming, saved_h, saved_u = loop_state
        micro_index = step_number - section_index
        in_range = (micro_index >= 0) & (micro_index < micro_count)
        which_micro = jnp.clip(micro_index, 0, micro_count - 1)
        fresh_rows = lax.dynamic_index_in_dim(tokens_in, which_micro, 0, keepdims=False)
        hidden = jnp.where(section_index == 0, fresh_rows, incoming)
        hidden = jnp.where(in_range, hidden, zero_value)
        route_ids = lax.dynamic_index_in_dim(layer_routes, which_micro, 0, keepdims=False)

        def run_forward(rows):
            return when_active(
                in_range, lambda values: expert_forward(values, own_in, own_out), rows
            )

        output, received = forward_layer(hidden, own_gain, own_router, route_ids, run_forward)
        saved_h = store_micro(saved_h, hidden, which_micro, in_range)
        saved_u = store_micro(saved_u, received, which_micro, in_range)
        outgoing = shifted(output, "pipe", 1)
        return (outgoing, saved_h, saved_u)

    final_rows, saved_h, saved_u = lax.fori_loop(
        0, total_steps, forward_step, (flat_zero, hidden_start, kept_start)
    )

    def backward_step(step_number, loop_state):
        incoming, records = loop_state
        micro_index = step_number - (sections - 1 - section_index)
        in_range = (micro_index >= 0) & (micro_index < micro_count)
        which_micro = jnp.clip(micro_index, 0, micro_count - 1)
        last_grad = lax.dynamic_index_in_dim(out_grad, which_micro, 0, keepdims=False)
        upstream = jnp.where(section_index == sections - 1, last_grad, incoming)
        upstream = jnp.where(in_range, upstream, zero_value)
        hidden = lax.dynamic_index_in_dim(saved_h, which_micro, 0, keepdims=False)
        route_ids = lax.dynamic_index_in_dim(layer_routes, which_micro, 0, keepdims=False)
        kept = lax.dynamic_index_in_dim(saved_u, which_micro, 0, keepdims=False)

        def run_backward(rows, grads, shares):
            return when_active(
                in_range,
                lambda packed: expert_backward(packed[0], packed[1], packed[2], own_in, own_out),
                (rows, grads, shares),
            )

        passed, record = backward_layer(
            hidden, upstream, own_gain, own_router, route_ids, kept, run_backward
        )
        records = tuple(
            (
                store_micro(stored, value, which_micro, in_range)
                for stored, value in zip(records, record)
            )
        )
        outgoing = shifted(passed, "pipe", -1)
        return (outgoing, records)

    final_grad, records = lax.fori_loop(0, total_steps, backward_step, (flat_zero, records_start))
    return weight_grads(
        records[0].reshape(-1, model_width),
        records[1].reshape(-1, 2 * inner_width),
        records[2].reshape(-1, inner_width),
        records[3].reshape(-1, model_width),
    )


def solution(mesh):
    placed = (
        P(None, "expert", None),
        P(None, "expert", None),
        P(None, None, "expert", None),
        P("pipe", None, None),
        P("pipe", None),
        P("pipe", "expert", None, None),
        P("pipe", "expert", None, None),
    )
    return jax.shard_map(
        shards,
        mesh=mesh,
        in_specs=placed,
        out_specs=(P("pipe", "expert", None, None), P("pipe", "expert", None, None)),
        check_vma=False,
    )
```

profile of v0, /device:TPU:1, one launch (start us, length us, event | category | flops | bytes accessed | tf_op | source)
XLA Modules:
  0.0 1651.5 jit_solution(9345934188295672058)
XLA Ops:
  6.4 714.7 %while.42 = (s32[]{:T(128)}, bf16[80,2048]{1,0:T(8,128)(2,1)}, bf16[2,80,2048]{2,1,0:T(8,128)(2,1)}, bf16[2,32,3,2048]{3,2,1,0:T(4,128)(2,1)}, s32[]{:T(128)}, /...) while((s32[]{:T(128)}, bf16[80,2048]{1,0:T(8,128)(2,1)}, ...), condition=%wide.region_9.10_spmd, body=%wide.region_0.9_spmd.sunk | while | flops 618040896 | bytes 25942808 | solution.py:265
  30.5 17.8 %all-to-all-done = bf16[32,3,2048]{2,1,0:T(4,128)(2,1)} async-done(((bf16[32,3,2048]{2,1,0:T(4,128)(2,1)}), bf16[32,3,2048]{2,1,0:T(4,128)(2,1)}, u32[]{:S(2)}, u32[]{:S(2)}) %all-to-all-start) | async-done | bytes 393248 | tf_op jit(solution)/shard_map/while/body/eval_jaxpr/all_to_all | solution.py:176
  62.6 16.2 all-to-all-done.1
  108.5 18.0 %all-to-all-done = bf16[32,3,2048]{2,1,0:T(4,128)(2,1)} async-done(((bf16[32,3,2048]{2,1,0:T(4,128)(2,1)}), bf16[32,3,2048]{2,1,0:T(4,128)(2,1)}, u32[]{:S(2)}, u32[]{:S(2)}) %all-to-all-start) | async-done | bytes 393248 | tf_op jit(solution)/shard_map/while/body/eval_jaxpr/all_to_all | solution.py:176
  140.8 16.2 all-to-all-done.1
  190.1 17.8 %all-to-all-done = bf16[32,3,2048]{2,1,0:T(4,128)(2,1)} async-done(((bf16[32,3,2048]{2,1,0:T(4,128)(2,1)}), bf16[32,3,2048]{2,1,0:T(4,128)(2,1)}, u32[]{:S(2)}, u32[]{:S(2)}) %all-to-all-start) | async-done | bytes 393248 | tf_op jit(solution)/shard_map/while/body/eval_jaxpr/all_to_all | solution.py:176
  217.4 16.2 all-to-all-done.1
  271.1 17.8 %all-to-all-done = bf16[32,3,2048]{2,1,0:T(4,128)(2,1)} async-done(((bf16[32,3,2048]{2,1,0:T(4,128)(2,1)}), bf16[32,3,2048]{2,1,0:T(4,128)(2,1)}, u32[]{:S(2)}, u32[]{:S(2)}) %all-to-all-start) | async-done | bytes 393248 | tf_op jit(solution)/shard_map/while/body/eval_jaxpr/all_to_all | solution.py:176
  298.4 16.2 all-to-all-done.1
  347.3 17.8 %all-to-all-done = bf16[32,3,2048]{2,1,0:T(4,128)(2,1)} async-done(((bf16[32,3,2048]{2,1,0:T(4,128)(2,1)}), bf16[32,3,2048]{2,1,0:T(4,128)(2,1)}, u32[]{:S(2)}, u32[]{:S(2)}) %all-to-all-start) | async-done | bytes 393248 | tf_op jit(solution)/shard_map/while/body/eval_jaxpr/all_to_all | solution.py:176
  374.6 16.2 all-to-all-done.1
  428.4 17.8 %all-to-all-done = bf16[32,3,2048]{2,1,0:T(4,128)(2,1)} async-done(((bf16[32,3,2048]{2,1,0:T(4,128)(2,1)}), bf16[32,3,2048]{2,1,0:T(4,128)(2,1)}, u32[]{:S(2)}, u32[]{:S(2)}) %all-to-all-start) | async-done | bytes 393248 | tf_op jit(solution)/shard_map/while/body/eval_jaxpr/all_to_all | solution.py:176
  455.7 16.2 all-to-all-done.1
  505.5 17.8 %all-to-all-done = bf16[32,3,2048]{2,1,0:T(4,128)(2,1)} async-done(((bf16[32,3,2048]{2,1,0:T(4,128)(2,1)}), bf16[32,3,2048]{2,1,0:T(4,128)(2,1)}, u32[]{:S(2)}, u32[]{:S(2)}) %all-to-all-start) | async-done | bytes 393248 | tf_op jit(solution)/shard_map/while/body/eval_jaxpr/all_to_all | solution.py:176
  532.8 16.2 all-to-all-done.1
  583.9 17.8 %all-to-all-done = bf16[32,3,2048]{2,1,0:T(4,128)(2,1)} async-done(((bf16[32,3,2048]{2,1,0:T(4,128)(2,1)}), bf16[32,3,2048]{2,1,0:T(4,128)(2,1)}, u32[]{:S(2)}, u32[]{:S(2)}) %all-to-all-start) | async-done | bytes 393248 | tf_op jit(solution)/shard_map/while/body/eval_jaxpr/all_to_all | solution.py:176
  611.2 16.2 all-to-all-done.1
  661.0 17.8 %all-to-all-done = bf16[32,3,2048]{2,1,0:T(4,128)(2,1)} async-done(((bf16[32,3,2048]{2,1,0:T(4,128)(2,1)}), bf16[32,3,2048]{2,1,0:T(4,128)(2,1)}, u32[]{:S(2)}, u32[]{:S(2)}) %all-to-all-start) | async-done | bytes 393248 | tf_op jit(solution)/shard_map/while/body/eval_jaxpr/all_to_all | solution.py:176
  688.3 16.2 all-to-all-done.1
  724.5 920.2 %while.43 = (s32[]{:T(128)}, bf16[80,2048]{1,0:T(8,128)(2,1)S(1)}, bf16[2,96,2048]{2,1,0:T(8,128)(2,1)}, bf16[2,96,1024]{2,1,0:T(8,128)(2,1)}, bf16[2,96,512]{2,...) while((s32[]{:T(128)}, bf16[80,2048]{1,0:T(8,128)(2,1)S(1)}, ...), condition=%wide.region_21.22_spmd, body=%wide.region_10.21_spmd.sunk | while | flops 1238116224 | bytes 73556168 | solution.py:300
  750.3 14.4 all-to-all-done.2
  835.6 14.4 all-to-all-done.2
  922.7 14.4 all-to-all-done.2
  1008.0 14.4 all-to-all-done.2
  1095.9 14.4 all-to-all-done.2
  1181.2 14.4 all-to-all-done.2
  1268.3 14.4 all-to-all-done.2
  1319.4 123.0 %collective-permute-done.1 = bf16[80,2048]{1,0:T(8,128)(2,1)S(1)} collective-permute-done((bf16[80,2048]{1,0:T(8,128)(2,1)S(1)}, bf16[80,2048]{1,0:T(8,128)(2,1)S(1)}, u32[]{:S(2)}, u32[]{:S(2)}) %collective-permute-start.1) | collective-permute-done | bytes 327712 | tf_op jit(solution)/shard_map/while/body/eval_jaxpr/ppermute | solution.py:27
  1468.0 14.4 all-to-all-done.2
  1482.4 19.0 %conditional.5 = (bf16[96,1024]{1,0:T(8,128)(2,1)S(1)}, bf16[96,512]{1,0:T(8,128)(2,1)}, bf16[96,2048]{1,0:T(8,128)(2,1)}, bf16[32,3,2048]{2,1,0:T(4,128)(2,1)}, bf16[32,3,1]{2,1,0:T(4,128)(2,1)S(1)}) conditional(s32[]{:T(128)} %convert_element_type.380, () %tuple.111, (bf16[32,3,2049]{2,1,0:T(4,128)(2,1)S(1)}, bf16[512,2048]{1,0:T(8,128)(2,1)S(1)}, ...), branch_computations={%region_17.17_spmd, %region_18.19_spmd} | conditional | flops 1210662912 | bytes 41749656 | solution.py:109
  1569.5 14.4 all-to-all-done.2
  1583.9 19.0 %conditional.5 = (bf16[96,1024]{1,0:T(8,128)(2,1)S(1)}, bf16[96,512]{1,0:T(8,128)(2,1)}, bf16[96,2048]{1,0:T(8,128)(2,1)}, bf16[32,3,2048]{2,1,0:T(4,128)(2,1)}, bf16[32,3,1]{2,1,0:T(4,128)(2,1)S(1)}) conditional(s32[]{:T(128)} %convert_element_type.380, () %tuple.111, (bf16[32,3,2049]{2,1,0:T(4,128)(2,1)S(1)}, bf16[512,2048]{1,0:T(8,128)(2,1)S(1)}, ...), branch_computations={%region_17.17_spmd, %region_18.19_spmd} | conditional | flops 1210662912 | bytes 41749656 | solution.py:109
  (1359 shorter events, 1113.1 us)
Async XLA Ops:
  17.6 30.8 %all-to-all-start = ((bf16[32,3,2048]{2,1,0:T(4,128)(2,1)}), bf16[32,3,2048]{2,1,0:T(4,128)(2,1)}, u32[]{:S(2)}, u32[]{:S(2)}) async-start(bf16[32,3,2048]{2,1,0:T(4,128)(2,1)} %broadcast_select_fusion.6), calls=%async_computation | async-start | bytes 1048576 | tf_op jit(solution)/shard_map/while/body/eval_jaxpr/all_to_all | solution.py:176
  54.3 24.5 %all-to-all-start.1 = ((bf16[32,3,2048]{2,1,0:T(4,128)(2,1)}), bf16[32,3,2048]{2,1,0:T(4,128)(2,1)}, u32[]{:S(2)}, u32[]{:S(2)}) async-start(bf16[32,3,2048]{2,1,0:T(4,128)(2,1)} %reshape.596), calls=%async_computation.1 | async-start | bytes 1048576 | tf_op jit(solution)/shard_map/while/body/eval_jaxpr/all_to_all | solution.py:179
  101.4 25.1 %all-to-all-start = ((bf16[32,3,2048]{2,1,0:T(4,128)(2,1)}), bf16[32,3,2048]{2,1,0:T(4,128)(2,1)}, u32[]{:S(2)}, u32[]{:S(2)}) async-start(bf16[32,3,2048]{2,1,0:T(4,128)(2,1)} %broadcast_select_fusion.6), calls=%async_computation | async-start | bytes 1048576 | tf_op jit(solution)/shard_map/while/body/eval_jaxpr/all_to_all | solution.py:176
  132.4 24.5 %all-to-all-start.1 = ((bf16[32,3,2048]{2,1,0:T(4,128)(2,1)}), bf16[32,3,2048]{2,1,0:T(4,128)(2,1)}, u32[]{:S(2)}, u32[]{:S(2)}) async-start(bf16[32,3,2048]{2,1,0:T(4,128)(2,1)} %reshape.596), calls=%async_computation.1 | async-start | bytes 1048576 | tf_op jit(solution)/shard_map/while/body/eval_jaxpr/all_to_all | solution.py:179
  182.1 25.9 %all-to-all-start = ((bf16[32,3,2048]{2,1,0:T(4,128)(2,1)}), bf16[32,3,2048]{2,1,0:T(4,128)(2,1)}, u32[]{:S(2)}, u32[]{:S(2)}) async-start(bf16[32,3,2048]{2,1,0:T(4,128)(2,1)} %broadcast_select_fusion.6), calls=%async_computation | async-start | bytes 1048576 | tf_op jit(solution)/shard_map/while/body/eval_jaxpr/all_to_all | solution.py:176
  209.0 24.5 %all-to-all-start.1 = ((bf16[32,3,2048]{2,1,0:T(4,128)(2,1)}), bf16[32,3,2048]{2,1,0:T(4,128)(2,1)}, u32[]{:S(2)}, u32[]{:S(2)}) async-start(bf16[32,3,2048]{2,1,0:T(4,128)(2,1)} %reshape.596), calls=%async_computation.1 | async-start | bytes 1048576 | tf_op jit(solution)/shard_map/while/body/eval_jaxpr/all_to_all | solution.py:179
  263.1 25.9 %all-to-all-start = ((bf16[32,3,2048]{2,1,0:T(4,128)(2,1)}), bf16[32,3,2048]{2,1,0:T(4,128)(2,1)}, u32[]{:S(2)}, u32[]{:S(2)}) async-start(bf16[32,3,2048]{2,1,0:T(4,128)(2,1)} %broadcast_select_fusion.6), calls=%async_computation | async-start | bytes 1048576 | tf_op jit(solution)/shard_map/while/body/eval_jaxpr/all_to_all | solution.py:176
  290.1 24.5 %all-to-all-start.1 = ((bf16[32,3,2048]{2,1,0:T(4,128)(2,1)}), bf16[32,3,2048]{2,1,0:T(4,128)(2,1)}, u32[]{:S(2)}, u32[]{:S(2)}) async-start(bf16[32,3,2048]{2,1,0:T(4,128)(2,1)} %reshape.596), calls=%async_computation.1 | async-start | bytes 1048576 | tf_op jit(solution)/shard_map/while/body/eval_jaxpr/all_to_all | solution.py:179
  339.3 25.9 %all-to-all-start = ((bf16[32,3,2048]{2,1,0:T(4,128)(2,1)}), bf16[32,3,2048]{2,1,0:T(4,128)(2,1)}, u32[]{:S(2)}, u32[]{:S(2)}) async-start(bf16[32,3,2048]{2,1,0:T(4,128)(2,1)} %broadcast_select_fusion.6), calls=%async_computation | async-start | bytes 1048576 | tf_op jit(solution)/shard_map/while/body/eval_jaxpr/all_to_all | solution.py:176
  366.2 24.5 %all-to-all-start.1 = ((bf16[32,3,2048]{2,1,0:T(4,128)(2,1)}), bf16[32,3,2048]{2,1,0:T(4,128)(2,1)}, u32[]{:S(2)}, u32[]{:S(2)}) async-start(bf16[32,3,2048]{2,1,0:T(4,128)(2,1)} %reshape.596), calls=%async_computation.1 | async-start | bytes 1048576 | tf_op jit(solution)/shard_map/while/body/eval_jaxpr/all_to_all | solution.py:179
  420.4 25.9 %all-to-all-start = ((bf16[32,3,2048]{2,1,0:T(4,128)(2,1)}), bf16[32,3,2048]{2,1,0:T(4,128)(2,1)}, u32[]{:S(2)}, u32[]{:S(2)}) async-start(bf16[32,3,2048]{2,1,0:T(4,128)(2,1)} %broadcast_select_fusion.6), calls=%async_computation | async-start | bytes 1048576 | tf_op jit(solution)/shard_map/while/body/eval_jaxpr/all_to_all | solution.py:176
  447.3 24.5 %all-to-all-start.1 = ((bf16[32,3,2048]{2,1,0:T(4,128)(2,1)}), bf16[32,3,2048]{2,1,0:T(4,128)(2,1)}, u32[]{:S(2)}, u32[]{:S(2)}) async-start(bf16[32,3,2048]{2,1,0:T(4,128)(2,1)} %reshape.596), calls=%async_computation.1 | async-start | bytes 1048576 | tf_op jit(solution)/shard_map/while/body/eval_jaxpr/all_to_all | solution.py:179
  497.5 25.9 %all-to-all-start = ((bf16[32,3,2048]{2,1,0:T(4,128)(2,1)}), bf16[32,3,2048]{2,1,0:T(4,128)(2,1)}, u32[]{:S(2)}, u32[]{:S(2)}) async-start(bf16[32,3,2048]{2,1,0:T(4,128)(2,1)} %broadcast_select_fusion.6), calls=%async_computation | async-start | bytes 1048576 | tf_op jit(solution)/shard_map/while/body/eval_jaxpr/all_to_all | solution.py:176
  524.4 24.5 %all-to-all-start.1 = ((bf16[32,3,2048]{2,1,0:T(4,128)(2,1)}), bf16[32,3,2048]{2,1,0:T(4,128)(2,1)}, u32[]{:S(2)}, u32[]{:S(2)}) async-start(bf16[32,3,2048]{2,1,0:T(4,128)(2,1)} %reshape.596), calls=%async_computation.1 | async-start | bytes 1048576 | tf_op jit(solution)/shard_map/while/body/eval_jaxpr/all_to_all | solution.py:179
  575.9 25.9 %all-to-all-start = ((bf16[32,3,2048]{2,1,0:T(4,128)(2,1)}), bf16[32,3,2048]{2,1,0:T(4,128)(2,1)}, u32[]{:S(2)}, u32[]{:S(2)}) async-start(bf16[32,3,2048]{2,1,0:T(4,128)(2,1)} %broadcast_select_fusion.6), calls=%async_computation | async-start | bytes 1048576 | tf_op jit(solution)/shard_map/while/body/eval_jaxpr/all_to_all | solution.py:176
  602.8 24.5 %all-to-all-start.1 = ((bf16[32,3,2048]{2,1,0:T(4,128)(2,1)}), bf16[32,3,2048]{2,1,0:T(4,128)(2,1)}, u32[]{:S(2)}, u32[]{:S(2)}) async-start(bf16[32,3,2048]{2,1,0:T(4,128)(2,1)} %reshape.596), calls=%async_computation.1 | async-start | bytes 1048576 | tf_op jit(solution)/shard_map/while/body/eval_jaxpr/all_to_all | solution.py:179
  653.0 25.9 %all-to-all-start = ((bf16[32,3,2048]{2,1,0:T(4,128)(2,1)}), bf16[32,3,2048]{2,1,0:T(4,128)(2,1)}, u32[]{:S(2)}, u32[]{:S(2)}) async-start(bf16[32,3,2048]{2,1,0:T(4,128)(2,1)} %broadcast_select_fusion.6), calls=%async_computation | async-start | bytes 1048576 | tf_op jit(solution)/shard_map/while/body/eval_jaxpr/all_to_all | solution.py:176
  679.9 24.5 %all-to-all-start.1 = ((bf16[32,3,2048]{2,1,0:T(4,128)(2,1)}), bf16[32,3,2048]{2,1,0:T(4,128)(2,1)}, u32[]{:S(2)}, u32[]{:S(2)}) async-start(bf16[32,3,2048]{2,1,0:T(4,128)(2,1)} %reshape.596), calls=%async_computation.1 | async-start | bytes 1048576 | tf_op jit(solution)/shard_map/while/body/eval_jaxpr/all_to_all | solution.py:179
  738.3 26.4 %all-to-all-start.2 = ((bf16[32,3,2049]{2,1,0:T(4,128)(2,1)}), bf16[32,3,2049]{2,1,0:T(4,128)(2,1)S(1)}, u32[]{:S(2)}, u32[]{:S(2)}) async-start(bf16[32,3,2049]{2,1,0:T(4,128)(2,1)} %pad_maximum_fusion.5), calls=%async_computation.2 | async-start | bytes 1114112 | tf_op jit(solution)/shard_map/while/body/eval_jaxpr/all_to_all | solution.py:13
  769.4 24.4 %all-to-all-start.3 = ((bf16[32,3,2049]{2,1,0:T(4,128)(2,1)}), bf16[32,3,2049]{2,1,0:T(4,128)(2,1)S(1)}, u32[]{:S(2)}, u32[]{:S(2)}) async-start(bf16[32,3,2049]{2,1,0:T(4,128)(2,1)} %pad_maximum_fusion.6), calls=%async_computation.3 | async-start | bytes 1114112 | tf_op jit(solution)/shard_map/while/body/eval_jaxpr/all_to_all | solution.py:13
  823.8 26.2 %all-to-all-start.2 = ((bf16[32,3,2049]{2,1,0:T(4,128)(2,1)}), bf16[32,3,2049]{2,1,0:T(4,128)(2,1)S(1)}, u32[]{:S(2)}, u32[]{:S(2)}) async-start(bf16[32,3,2049]{2,1,0:T(4,128)(2,1)} %pad_maximum_fusion.5), calls=%async_computation.2 | async-start | bytes 1114112 | tf_op jit(solution)/shard_map/while/body/eval_jaxpr/all_to_all | solution.py:13
  910.9 26.2 %all-to-all-start.2 = ((bf16[32,3,2049]{2,1,0:T(4,128)(2,1)}), bf16[32,3,2049]{2,1,0:T(4,128)(2,1)S(1)}, u32[]{:S(2)}, u32[]{:S(2)}) async-start(bf16[32,3,2049]{2,1,0:T(4,128)(2,1)} %pad_maximum_fusion.5), calls=%async_computation.2 | async-start | bytes 1114112 | tf_op jit(solution)/shard_map/while/body/eval_jaxpr/all_to_all | solution.py:13
  996.1 26.2 %all-to-all-start.2 = ((bf16[32,3,2049]{2,1,0:T(4,128)(2,1)}), bf16[32,3,2049]{2,1,0:T(4,128)(2,1)S(1)}, u32[]{:S(2)}, u32[]{:S(2)}) async-start(bf16[32,3,2049]{2,1,0:T(4,128)(2,1)} %pad_maximum_fusion.5), calls=%async_computation.2 | async-start | bytes 1114112 | tf_op jit(solution)/shard_map/while/body/eval_jaxpr/all_to_all | solution.py:13
  1027.1 24.4 %all-to-all-start.3 = ((bf16[32,3,2049]{2,1,0:T(4,128)(2,1)}), bf16[32,3,2049]{2,1,0:T(4,128)(2,1)S(1)}, u32[]{:S(2)}, u32[]{:S(2)}) async-start(bf16[32,3,2049]{2,1,0:T(4,128)(2,1)} %pad_maximum_fusion.6), calls=%async_computation.3 | async-start | bytes 1114112 | tf_op jit(solution)/shard_map/while/body/eval_jaxpr/all_to_all | solution.py:13
  1084.1 26.2 %all-to-all-start.2 = ((bf16[32,3,2049]{2,1,0:T(4,128)(2,1)}), bf16[32,3,2049]{2,1,0:T(4,128)(2,1)S(1)}, u32[]{:S(2)}, u32[]{:S(2)}) async-start(bf16[32,3,2049]{2,1,0:T(4,128)(2,1)} %pad_maximum_fusion.5), calls=%async_computation.2 | async-start | bytes 1114112 | tf_op jit(solution)/shard_map/while/body/eval_jaxpr/all_to_all | solution.py:13
  1169.4 26.2 %all-to-all-start.2 = ((bf16[32,3,2049]{2,1,0:T(4,128)(2,1)}), bf16[32,3,2049]{2,1,0:T(4,128)(2,1)S(1)}, u32[]{:S(2)}, u32[]{:S(2)}) async-start(bf16[32,3,2049]{2,1,0:T(4,128)(2,1)} %pad_maximum_fusion.5), calls=%async_computation.2 | async-start | bytes 1114112 | tf_op jit(solution)/shard_map/while/body/eval_jaxpr/all_to_all | solution.py:13
  1256.5 26.2 %all-to-all-start.2 = ((bf16[32,3,2049]{2,1,0:T(4,128)(2,1)}), bf16[32,3,2049]{2,1,0:T(4,128)(2,1)S(1)}, u32[]{:S(2)}, u32[]{:S(2)}) async-start(bf16[32,3,2049]{2,1,0:T(4,128)(2,1)} %pad_maximum_fusion.5), calls=%async_computation.2 | async-start | bytes 1114112 | tf_op jit(solution)/shard_map/while/body/eval_jaxpr/all_to_all | solution.py:13
  1287.4 24.4 %all-to-all-start.3 = ((bf16[32,3,2049]{2,1,0:T(4,128)(2,1)}), bf16[32,3,2049]{2,1,0:T(4,128)(2,1)S(1)}, u32[]{:S(2)}, u32[]{:S(2)}) async-start(bf16[32,3,2049]{2,1,0:T(4,128)(2,1)} %pad_maximum_fusion.6), calls=%async_computation.3 | async-start | bytes 1114112 | tf_op jit(solution)/shard_map/while/body/eval_jaxpr/all_to_all | solution.py:13
  1317.9 124.4 %collective-permute-start.1 = (bf16[80,2048]{1,0:T(8,128)(2,1)S(1)}, bf16[80,2048]{1,0:T(8,128)(2,1)S(1)}, u32[]{:S(2)}, u32[]{:S(2)}) collective-permute-start(bf16[80,2048]{1,0:T(8,128)(2,1)S(1)} %fusion.126), channel_id=1, source_target_pairs={{32,0},{64,32},{96,64},{128,96},{160,128},{192,160},{224,192},{33,... | collective-permute-start | bytes 983048 | tf_op jit(solution)/shard_map/while/body/eval_jaxpr/ppermute | solution.py:27
  1456.2 26.2 %all-to-all-start.2 = ((bf16[32,3,2049]{2,1,0:T(4,128)(2,1)}), bf16[32,3,2049]{2,1,0:T(4,128)(2,1)S(1)}, u32[]{:S(2)}, u32[]{:S(2)}) async-start(bf16[32,3,2049]{2,1,0:T(4,128)(2,1)} %pad_maximum_fusion.5), calls=%async_computation.2 | async-start | bytes 1114112 | tf_op jit(solution)/shard_map/while/body/eval_jaxpr/all_to_all | solution.py:13
  1503.6 24.4 %all-to-all-start.3 = ((bf16[32,3,2049]{2,1,0:T(4,128)(2,1)}), bf16[32,3,2049]{2,1,0:T(4,128)(2,1)S(1)}, u32[]{:S(2)}, u32[]{:S(2)}) async-start(bf16[32,3,2049]{2,1,0:T(4,128)(2,1)} %pad_maximum_fusion.6), calls=%async_computation.3 | async-start | bytes 1114112 | tf_op jit(solution)/shard_map/while/body/eval_jaxpr/all_to_all | solution.py:13
  1557.7 26.2 %all-to-all-start.2 = ((bf16[32,3,2049]{2,1,0:T(4,128)(2,1)}), bf16[32,3,2049]{2,1,0:T(4,128)(2,1)S(1)}, u32[]{:S(2)}, u32[]{:S(2)}) async-start(bf16[32,3,2049]{2,1,0:T(4,128)(2,1)} %pad_maximum_fusion.5), calls=%async_computation.2 | async-start | bytes 1114112 | tf_op jit(solution)/shard_map/while/body/eval_jaxpr/all_to_all | solution.py:13
  (241 other events, 2362.1 us)
where the time goes:
time: 1660 us; the launch traced here: 1650 us
  waiting for transfers between devices  776 us (47%)
  local copies, waits for them, and re-layouts  315 us (19%)
  starting transfers between devices  308 us (19%)
  other arithmetic  179 us (11%)
  matrix products  65.3 us (4%)
    all_to_all x18, waiting for transfers between devices, side_by_side(): lax.all_to_all(both, axis, split_axis=split_dim, concat_axis=concat_dim,...  251 us
    ppermute x18, waiting for transfers between devices, shifted(): return lax.ppermute(block, axis, route)  219 us
    all_to_all x9, waiting for transfers between devices, forward_layer(): lax.all_to_all(send_rows, 'expert', split_axis=0, concat_axis=0, tiled=True)  161 us
    all_to_all x9, waiting for transfers between devices, forward_layer(): lax.all_to_all(produced.reshape(rank_count, part_slots, model_width), 'ex...  145 us
    all_to_all x18, starting transfers between devices, side_by_side(): lax.all_to_all(both, axis, split_axis=split_dim, concat_axis=concat_dim,...  118 us
    all_to_all x9, starting transfers between devices, forward_layer(): lax.all_to_all(send_rows, 'expert', split_axis=0, concat_axis=0, tiled=True)  73.5 us
    gather x45, local copies, waits for them, and re-layouts, to_slots(): gathered = source[index_table]  71 us
    ppermute x18, starting transfers between devices, shifted(): return lax.ppermute(block, axis, route)  60.2 us
  transfers between devices with their start and end apart: 54, of which 54 were waited for; matrix products, arithmetic and copies ran while one was open for 8% of the time, Pallas kernels for 0%

commit v1 on v0

v1 whole, which is shorter than its diff:
```python
import functools

import jax
import jax.numpy as jnp
from jax import lax
from jax.experimental import pallas as pl
from jax.experimental.pallas import tpu as pltpu
from jax.sharding import PartitionSpec as P

epsilon = 1e-06
CAP = 3
GROUPS = 2
LANES = 128
F32 = jnp.float32
BF16 = jnp.bfloat16
MESH = pl.DeviceIdType.MESH
NT = (((1,), (1,)), ((), ()))


def wide(value):
    return jnp.broadcast_to(value, (value.shape[0], LANES))


def relay(
    stages,
    ranks,
    micros,
    tokens,
    tables,
    source,
    gain,
    column,
    w_in_any,
    w_out_any,
    normed_out,
    joined_out,
    act_out,
    scaled_out,
    w_in,
    w_out,
    flat,
    staging,
    home_f_in,
    home_b_in,
    home_f_out,
    home_b_out,
    land_f,
    land_b,
    leave_f,
    leave_b,
    hidden,
    gate_part,
    up_part,
    produced,
    prob_kept,
    inverse_kept,
    up_grad,
    mixed,
    sems,
    weight_sems,
):
    chunks = micros * GROUPS
    slots = ranks * CAP
    homes = ranks // GROUPS
    rows = homes * CAP
    width = hidden.shape[2]
    tiles = width // LANES
    inner = w_out.shape[0]
    stage = lax.axis_index("pipe")
    me = lax.axis_index("expert")
    last = stages - 1
    my_group = lax.rem(me, GROUPS)
    my_place = lax.div(me, GROUPS)

    load_in = pltpu.make_async_copy(w_in_any.at[0, 0], w_in, weight_sems.at[0])
    load_out = pltpu.make_async_copy(w_out_any.at[0, 0], w_out, weight_sems.at[1])
    load_in.start()
    load_out.start()
    staging[slots] = jnp.zeros(staging.shape[1:], BF16)

    def drain(ref, sem):
        pltpu.make_async_copy(ref, ref, sem).wait()

    def home(chunk, table_row, at_source, came, came_sem, out, out_sem, land, land_sem):
        micro = lax.div(chunk, GROUPS)

        @pl.when(at_source)
        def _():
            staging[0:tokens] = source[micro]

        @pl.when(jnp.logical_not(at_source))
        def _():
            drain(came.at[micro], came_sem.at[micro])
            staging[0:slots] = came[micro]

        base = (table_row * micros + micro) * slots

        def place(step, carry):
            for inside in range(CAP):
                slot = step * CAP + inside
                out[micro, slot] = staging[tables[base + slot]]
            return carry

        lax.fori_loop(0, ranks, place, 0)
        mine = land.at[chunk, pl.ds(my_place * CAP, CAP)]
        pltpu.make_async_copy(
            out.at[micro, pl.ds(me * CAP, CAP)], mine, land_sem.at[chunk]
        ).start()

        def send(step, carry):
            peer = lax.rem(me + step, ranks)
            pltpu.make_async_remote_copy(
                src_ref=out.at[micro, pl.ds(peer * CAP, CAP)],
                dst_ref=mine,
                send_sem=out_sem.at[micro],
                recv_sem=land_sem.at[chunk],
                device_id={"pipe": stage, "expert": peer},
                device_id_type=MESH,
            ).start()
            return carry

        lax.fori_loop(1, ranks, send, 0)

    def send_home(chunk, to_stage, leave, leave_sem, came, came_sem):
        micro = lax.div(chunk, GROUPS)
        group = lax.rem(chunk, GROUPS)

        def send(step, carry):
            place = lax.rem(my_place + step, homes)
            pltpu.make_async_remote_copy(
                src_ref=leave.at[chunk, pl.ds(place * CAP, CAP)],
                dst_ref=came.at[micro, pl.ds(me * CAP, CAP)],
                send_sem=leave_sem.at[chunk],
                recv_sem=came_sem.at[micro],
                device_id={"pipe": to_stage, "expert": place * GROUPS + group},
                device_id_type=MESH,
            ).start()
            return carry

        lax.fori_loop(0, homes, send, 0)

    def spread(chunk, land):
        flat[...] = land[chunk].astype(F32).reshape(rows * tiles, LANES)

    def gather_rows(chunk, leave):
        leave[chunk] = flat[...].reshape(rows, tiles, LANES).astype(BF16)

    def strip(at):
        return pl.ds(at * LANES, LANES)

    def tile_rows(at):
        return pl.ds(at, rows, stride=tiles)

    def forward(chunk):
        drain(land_f.at[chunk], sems.at[1].at[chunk])
        spread(chunk, land_f)
        squares = jnp.zeros((rows, LANES), F32)
        for at in range(tiles):
            piece = flat[tile_rows(at), :]
            hidden[chunk, :, strip(at)] = piece
            squares += piece * piece
        inverse = lax.rsqrt(jnp.sum(squares, axis=1, keepdims=True) / width + epsilon)
        inverse = wide(inverse)
        inverse_kept[chunk] = inverse
        scores = jnp.zeros((rows, LANES), F32)
        for at in range(tiles):
            piece = hidden[chunk, :, strip(at)] * inverse * gain[:, strip(at)]
            piece = piece.astype(BF16)
            normed_out[chunk, :, strip(at)] = piece
            scores += piece.astype(F32) * column[:, strip(at)]
        prob = wide(jax.nn.sigmoid(jnp.sum(scores, axis=1, keepdims=True)))
        prob_kept[chunk] = prob
        share = prob.astype(BF16).astype(F32)
        normed = normed_out[chunk]
        block = min(256, inner)
        for at in range(inner // block):
            cols = pl.ds(at * block, block)
            g = jnp.dot(normed, w_in[:, cols], preferred_element_type=F32)
            u = jnp.dot(
                normed, w_in[:, pl.ds(inner + at * block, block)], preferred_element_type=F32
            )
            gate_part[chunk, :, cols] = g
            up_part[chunk, :, cols] = u
            act_out[chunk, :, cols] = (g * jax.nn.sigmoid(g) * u).astype(BF16)
        activated = act_out[chunk]
        block = min(256, width)
        for at in range(width // block):
            cols = pl.ds(at * block, block)
            result = jnp.dot(activated, w_out[:, cols], preferred_element_type=F32).astype(BF16)
            produced[chunk, :, cols] = result
            for inside in range(block // LANES):
                tile = at * (block // LANES) + inside
                piece = result[:, inside * LANES : (inside + 1) * LANES].astype(F32)
                flat[tile_rows(tile), :] = hidden[chunk, :, strip(tile)] + share * piece

        @pl.when(stage < last)
        def _():
            gather_rows(chunk, leave_f)
            send_home(chunk, stage + 1, leave_f, sems.at[2], home_f_in, sems.at[0])

    def backward(chunk):
        drain(land_b.at[chunk], sems.at[5].at[chunk])
        spread(chunk, land_b)
        prob = prob_kept[chunk]
        share = prob.astype(BF16).astype(F32)
        sums = jnp.zeros((rows, LANES), F32)
        for at in range(tiles):
            piece = flat[tile_rows(at), :]
            up_grad[:, strip(at)] = piece
            sums += produced[chunk, :, strip(at)].astype(F32) * piece
            scaled_out[chunk, :, strip(at)] = (share * piece).astype(BF16)
        share_grad = jnp.sum(sums, axis=1, keepdims=True).astype(BF16).astype(F32)
        logit_grad = wide(share_grad) * prob * (1.0 - prob)
        scaled_grad = scaled_out[chunk]
        block = min(256, inner)
        for at in range(inner // block):
            cols = pl.ds(at * block, block)
            act_grad = lax.dot_general(scaled_grad, w_out[cols, :], NT, preferred_element_type=F32)
            g = gate_part[chunk, :, cols]
            u = up_part[chunk, :, cols]
            s = jax.nn.sigmoid(g)
            joined_out[chunk, :, cols] = (act_grad * u * s * (1.0 + g * (1.0 - s))).astype(BF16)
            joined_out[chunk, :, pl.ds(inner + at * block, block)] = (act_grad * (g * s)).astype(
                BF16
            )

        @pl.when(stage > 0)
        def _():
            joined = joined_out[chunk]
            inverse = inverse_kept[chunk]
            wide_block = min(256, width)
            total = jnp.zeros((rows, LANES), F32)
            for at in range(width // wide_block):
                cols = pl.ds(at * wide_block, wide_block)
                result = lax.dot_general(joined, w_in[cols, :], NT, preferred_element_type=F32)
                for inside in range(wide_block // LANES):
                    tile = at * (wide_block // LANES) + inside
                    piece = result[:, inside * LANES : (inside + 1) * LANES]
                    piece = piece.astype(BF16).astype(F32) + logit_grad * column[:, strip(tile)]
                    piece = piece * gain[:, strip(tile)]
                    mixed[:, strip(tile)] = piece
                    total += piece * (hidden[chunk, :, strip(tile)] * inverse)
            mean = wide(jnp.sum(total, axis=1, keepdims=True) / width)
            for at in range(tiles):
                scaled = hidden[chunk, :, strip(at)] * inverse
                centred = mixed[:, strip(at)] - scaled * mean
                flat[tile_rows(at), :] = up_grad[:, strip(at)] + inverse * centred
            gather_rows(chunk, leave_b)
            send_home(chunk, stage - 1, leave_b, sems.at[6], home_b_in, sems.at[4])

    is_last = stage == last

    def step(turn, carry):
        @pl.when((turn < chunks) & (lax.rem(turn, GROUPS) == my_group))
        def _():
            home(
                turn, 0, stage == 0, home_f_in, sems.at[0],
                home_f_out, sems.at[3], land_f, sems.at[1],
            )

        @pl.when(turn == 1)
        def _():
            load_in.wait()
            load_out.wait()

        @pl.when((turn >= 1) & (turn <= chunks))
        def _():
            forward(turn - 1)

        back = jnp.where(is_last, turn, turn - chunks)

        @pl.when((back >= 0) & (back < chunks) & (lax.rem(back + chunks, GROUPS) == my_group))
        def _():
            home(
                back, 1, is_last, home_b_in, sems.at[4],
                home_b_out, sems.at[7], land_b, sems.at[5],
            )

        @pl.when((back >= 1) & (back <= chunks))
        def _():
            backward(back - 1)

        return carry

    lax.fori_loop(0, 2 * chunks + 1, step, 0)

    for micro in range(micros):
        away = pl.ds(0, slots - CAP)
        drain(home_f_out.at[micro, away], sems.at[3].at[micro])
        drain(home_b_out.at[micro, away], sems.at[7].at[micro])

    @pl.when(stage < last)
    def _():
        for chunk in range(chunks):
            drain(leave_f.at[chunk], sems.at[2].at[chunk])

    @pl.when(stage > 0)
    def _():
        for chunk in range(chunks):
            drain(leave_b.at[chunk], sems.at[6].at[chunk])


def row_tables(routes, stage, stages, slots):
    ids = routes[..., 0]

    def positions(layer):
        own = lax.dynamic_index_in_dim(ids, layer, 0, keepdims=False)
        order = jnp.arange(own.shape[1], dtype=jnp.int32)
        before = order[:, None] > order[None, :]
        same = (own[:, :, None] == own[:, None, :]) & before[None]
        return own * CAP + jnp.sum(same.astype(jnp.int32), axis=2)

    here = positions(stage)
    token = jnp.broadcast_to(jnp.arange(here.shape[1], dtype=jnp.int32)[None], here.shape)
    below = jnp.where(stage == 0, token, positions(jnp.maximum(stage - 1, 0)))
    above = jnp.where(stage == stages - 1, token, positions(jnp.minimum(stage + 1, stages - 1)))
    places = jnp.arange(slots, dtype=jnp.int32)
    hit = here[:, :, None] == places[None, None, :]
    pairs = jnp.stack([below, above])
    table = slots + jnp.sum(jnp.where(hit[None], pairs[..., None] - slots, 0), axis=2)
    return table.reshape(-1)


def weight_grad(left, right):
    dims = (((0, 1), (0, 1)), ((), ()))
    return lax.dot_general(left, right, dims, preferred_element_type=F32).astype(BF16)[None, None]


def shards(tokens_in, out_grad, routes, router, norm_gain, w_in, w_out):
    stages = lax.axis_size("pipe")
    ranks = lax.axis_size("expert")
    stage = lax.axis_index("pipe")
    me = lax.axis_index("expert")
    micros, tokens, width = tokens_in.shape
    inner = w_out.shape[2]
    tiles = width // LANES
    slots = ranks * CAP
    chunks = micros * GROUPS
    rows = slots // GROUPS
    source = jnp.where(stage == stages - 1, out_grad, tokens_in)
    source = source.reshape(micros, tokens, tiles, LANES)
    tables = row_tables(routes, stage, stages, slots)
    chosen = (jnp.arange(ranks, dtype=jnp.int32) == me).astype(BF16)[None]
    column = lax.dot_general(chosen, router[0], NT, preferred_element_type=F32)
    gain = norm_gain.astype(F32)

    vmem = pl.BlockSpec(memory_space=pltpu.VMEM)
    anywhere = pl.BlockSpec(memory_space=pl.ANY)
    parts = pl.pallas_call(
        functools.partial(relay, stages, ranks, micros, tokens),
        out_shape=(
            jax.ShapeDtypeStruct((chunks, rows, width), BF16),
            jax.ShapeDtypeStruct((chunks, rows, 2 * inner), BF16),
            jax.ShapeDtypeStruct((chunks, rows, inner), BF16),
            jax.ShapeDtypeStruct((chunks, rows, width), BF16),
        ),
        in_specs=[
            pl.BlockSpec(memory_space=pltpu.SMEM), vmem, vmem, vmem, anywhere, anywhere,
        ],
        out_specs=(vmem, vmem, vmem, vmem),
        scratch_shapes=[
            pltpu.VMEM((width, 2 * inner), BF16),
            pltpu.VMEM((inner, width), BF16),
            pltpu.VMEM((rows * tiles, LANES), F32),
            pltpu.VMEM((slots + 1, tiles, LANES), BF16),
            *[pltpu.VMEM((micros, slots, tiles, LANES), BF16)] * 4,
            *[pltpu.VMEM((chunks, rows, tiles, LANES), BF16)] * 4,
            pltpu.VMEM((chunks, rows, width), F32),
            pltpu.VMEM((chunks, rows, inner), F32),
            pltpu.VMEM((chunks, rows, inner), F32),
            pltpu.VMEM((chunks, rows, width), BF16),
            pltpu.VMEM((chunks, rows, LANES), F32),
            pltpu.VMEM((chunks, rows, LANES), F32),
            pltpu.VMEM((rows, width), F32),
            pltpu.VMEM((rows, width), F32),
            pltpu.SemaphoreType.DMA((8, chunks)),
            pltpu.SemaphoreType.DMA((2,)),
        ],
        compiler_params=pltpu.CompilerParams(
            has_side_effects=True, vmem_limit_bytes=56 * 1024 * 1024
        ),
        name="relay",
    )(tables, source, gain, column, w_in, w_out)
    normed, joined, activated, scaled = parts
    return (weight_grad(normed, joined), weight_grad(activated, scaled))


def solution(mesh):
    placed = (
        P(None, "expert", None),
        P(None, "expert", None),
        P(None, None, "expert", None),
        P("pipe", None, None),
        P("pipe", None),
        P("pipe", "expert", None, None),
        P("pipe", "expert", None, None),
    )
    return jax.shard_map(
        shards,
        mesh=mesh,
        in_specs=placed,
        out_specs=(P("pipe", "expert", None, None), P("pipe", "expert", None, None)),
        check_vma=False,
    )
```

time: 1660 us -> 415 us (0.25)
  waiting for transfers between devices: 776 us -> 0 us
  Pallas kernels: 0 us -> 400 us
  local copies, waits for them, and re-layouts: 315 us -> 3.07 us
  starting transfers between devices: 308 us -> 0 us
  other arithmetic: 179 us -> 3.7 us
  matrix products: 65.3 us -> 7.42 us
    all_to_all x36 -> x0, waiting for transfers between devices: 557 us -> none  [the longest x18 251 us: side_by_side(): lax.all_to_all(both, axis, split_axis=split_dim, concat_axis=concat_dim,...]
    pallas_call x0 -> x1, Pallas kernels: none -> 400 us  [shards(): pl.pallas_call(functools.partial(relay, stages, ranks, micros, tokens), o...]
    all_to_all x36 -> x0, starting transfers between devices: 248 us -> none  [the longest x18 118 us: side_by_side(): lax.all_to_all(both, axis, split_axis=split_dim, concat_axis=concat_dim,...]
    ppermute x18 -> x0, waiting for transfers between devices: 219 us -> none  [shifted(): return lax.ppermute(block, axis, route)]
    gather x72 -> x0, local copies, waits for them, and re-layouts: 103 us -> none  [the longest x45 71 us: to_slots(): gathered = source[index_table]]
    dynamic_slice x54 -> x1, local copies, waits for them, and re-layouts: 75.5 us -> 0.72 us  [positions(): own = lax.dynamic_index_in_dim(ids, layer, 0, keepdims=False)]
    reshape x74 -> x0, local copies, waits for them, and re-layouts: 68.6 us -> none  [the longest x11 21.3 us: backward_layer(): flat_rows = kept_rows.reshape(-1, model_width)]
    ppermute x18 -> x0, starting transfers between devices: 60.2 us -> none  [shifted(): return lax.ppermute(block, axis, route)]
  transfers between devices with their start and end apart: 54 -> 0, of which waited for: 54 -> 0; matrix products, arithmetic and copies ran while one was open for 8% -> 0% of each run, Pallas kernels for 0% -> 0%
where the time goes in v1:
time: 415 us
  Pallas kernels  400 us (96%)
  matrix products  7.42 us (2%)
    pallas_call x1, Pallas kernels, shards(): pl.pallas_call(functools.partial(relay, stages, ranks, micros, tokens), o...  400 us

profile of v1, /device:TPU:1, one launch (start us, length us, event | category | flops | bytes accessed | tf_op | source)
XLA Modules:
  0.0 414.6 jit_solution(10137369310544646800)
XLA Ops:
  0.6 0.0 copy-start
  0.6 0.7 constant_dynamic-slice_fusion.2
  1.4 0.7 fusion.11
  2.1 0.3 convert_reduce_fusion.2
  2.4 0.7 fusion.9
  3.1 0.1 iota_compare_fusion
  3.2 0.1 select_reduce_fusion
  3.3 0.7 add.57.tables
  4.0 1.2 broadcast_select_fusion
  5.2 1.0 copy.13
  6.1 1.3 convert_element_type.22.gain
  7.4 0.0 copy-done
  7.4 0.7 fusion.2.column
  8.2 399.7 %relay.1 = (bf16[4,48,2048]{2,1,0:T(8,128)(2,1)}, bf16[4,48,1024]{2,1,0:T(8,128)(2,1)}, bf16[4,48,512]{2,1,0:T(8,128)(2,1)}, bf16[4,48,2048]{2,1,0:T(8,128)(2,1)}) custom-call(s32[384]{0:T(512)} %add.57.tables, bf16[2,80,16,128]{3,2,1,0:T(8,128)(2,1)} %bitcast.50, f32[1,2048]{1,0:T(1,128)} %convert_element_type.22.gain, f32[1,2048]{1,0:T(1,128)} %fusion.2.column, ...), custom_call_target="tpu_custom_call" | custom-call | tf_op jit(solution)/shard_map/relay/pallas_call | solution.py:349
  407.9 0.0 copy-start.1
  407.9 0.0 copy-start.2
  407.9 4.6 %fusion = bf16[1,1,2048,1024]{3,2,1,0:T(8,128)(2,1)} fusion(bf16[4,48,2048]{2,1,0:T(8,128)(2,1)} %get-tuple-element.6, bf16[4,48,1024]{2,1,0:T(8,128)(2,1)} %get-tuple-element.7), kind=kOutput, calls=%fused_computation.2 | convolution fusion | flops 807403520 | bytes 5373952 | tf_op jit(solution)/shard_map/dot_general | solution.py:326
  412.5 0.0 copy-done.1
  412.5 0.0 copy-done.2
  412.5 2.1 fusion.1
  (4 shorter events, 0.0 us)
Async XLA Ops:
  0.6 6.8 %copy-start = (bf16[1,2048,32]{1,2,0:T(8,128)(2,1)S(1)}, bf16[1,2048,32]{1,2,0:T(8,128)(2,1)}, u32[]{:S(2)}) copy-start(bf16[1,2048,32]{1,2,0:T(8,128)(2,1)} %param.10) | copy-start | bytes 393220
  407.9 4.6 %copy-start.1 = (bf16[4,48,2048]{2,1,0:T(8,128)(2,1)S(1)}, bf16[4,48,2048]{2,1,0:T(8,128)(2,1)}, u32[]{:S(2)}) copy-start(bf16[4,48,2048]{2,1,0:T(8,128)(2,1)} %get-tuple-element.9) | copy-start | bytes 2359300
  407.9 4.6 %copy-start.2 = (bf16[4,48,512]{2,1,0:T(8,128)(2,1)S(1)}, bf16[4,48,512]{2,1,0:T(8,128)(2,1)}, u32[]{:S(2)}) copy-start(bf16[4,48,512]{2,1,0:T(8,128)(2,1)} %get-tuple-element.8) | copy-start | bytes 589828

commit v2 on v1

--- a/solution.py
+++ b/solution.py
@@ -9,7 +9,8 @@
 
 epsilon = 1e-06
 CAP = 3
-GROUPS = 2
+GROUPS = 4
+PACE = 8
 LANES = 128
 F32 = jnp.float32
 BF16 = jnp.bfloat16
@@ -28,7 +29,7 @@
     tokens,
     tables,
     source,
-    gain,
+    gain_given,
     column,
     w_in_any,
     w_out_any,
@@ -56,6 +57,7 @@
     inverse_kept,
     up_grad,
     mixed,
+    gain,
     sems,
     weight_sems,
 ):
@@ -78,10 +80,24 @@
     load_out.start()
     staging[slots] = jnp.zeros(staging.shape[1:], BF16)
 
+    ring = ranks // 4
+    my_ring = lax.rem(lax.div(me, 2), ring)
+
+    def neighbour(step, inside):
+        half = lax.div(step + 1, 2)
+        away = jnp.where(lax.rem(step, 2) == 1, ring // 2 + half, ring // 2 + ring - half)
+        side = lax.rem(lax.div(me, 2 * ring) + inside // 2, 2)
+        core = lax.rem(me + inside, 2)
+        return (side * ring + lax.rem(my_ring + away, ring)) * 2 + core
+
+    gain[...] = gain_given[...].astype(F32)
+
     def drain(ref, sem):
         pltpu.make_async_copy(ref, ref, sem).wait()
 
-    def home(chunk, table_row, at_source, came, came_sem, out, out_sem, land, land_sem):
+    def home(
+        chunk, table_row, to_stage, at_source, pace, came, came_sem, out, out_sem, land, land_sem
+    ):
         micro = lax.div(chunk, GROUPS)
 
         @pl.when(at_source)
@@ -101,43 +117,52 @@
                 out[micro, slot] = staging[tables[base + slot]]
             return carry
 
-        lax.fori_loop(0, ranks, place, 0)
+        def again(step, carry):
+            lax.fori_loop(0, ranks, place, 0)
+            return carry
+
+        lead = jnp.where(chunk < GROUPS, chunk, GROUPS)
+        lax.fori_loop(0, jnp.where(at_source, 1 + pace * lead, 1), again, 0)
         mine = land.at[chunk, pl.ds(my_place * CAP, CAP)]
-        pltpu.make_async_copy(
-            out.at[micro, pl.ds(me * CAP, CAP)], mine, land_sem.at[chunk]
-        ).start()
 
         def send(step, carry):
-            peer = lax.rem(me + step, ranks)
-            pltpu.make_async_remote_copy(
-                src_ref=out.at[micro, pl.ds(peer * CAP, CAP)],
-                dst_ref=mine,
-                send_sem=out_sem.at[micro],
-                recv_sem=land_sem.at[chunk],
-                device_id={"pipe": stage, "expert": peer},
-                device_id_type=MESH,
-            ).start()
+            for inside in (3, 2, 1, 0):
+                peer = neighbour(step, inside)
+                pltpu.make_async_remote_copy(
+                    src_ref=out.at[micro, pl.ds(peer * CAP, CAP)],
+                    dst_ref=mine,
+                    send_sem=out_sem.at[micro],
+                    recv_sem=land_sem.at[chunk],
+                    device_id={"pipe": to_stage, "expert": peer},
+                    device_id_type=MESH,
+                ).start()
             return carry
 
-        lax.fori_loop(1, ranks, send, 0)
+        lax.fori_loop(0, ring, send, 0)
 
     def send_home(chunk, to_stage, leave, leave_sem, came, came_sem):
         micro = lax.div(chunk, GROUPS)
         group = lax.rem(chunk, GROUPS)
 
+        zs = homes // 2
+
         def send(step, carry):
-            place = lax.rem(my_place + step, homes)
-            pltpu.make_async_remote_copy(
-                src_ref=leave.at[chunk, pl.ds(place * CAP, CAP)],
-                dst_ref=came.at[micro, pl.ds(me * CAP, CAP)],
-                send_sem=leave_sem.at[chunk],
-                recv_sem=came_sem.at[micro],
-                device_id={"pipe": to_stage, "expert": place * GROUPS + group},
-                device_id_type=MESH,
-            ).start()
+            half = lax.div(step + 1, 2)
+            away = jnp.where(lax.rem(step, 2) == 1, zs // 2 + half, zs // 2 + zs - half)
+            z = lax.rem(lax.rem(my_place, zs) + away, zs)
+            for inside in (1, 0):
+                place = lax.rem(lax.div(my_place, zs) + inside, 2) * zs + z
+                pltpu.make_async_remote_copy(
+                    src_ref=leave.at[chunk, pl.ds(place * CAP, CAP)],
+                    dst_ref=came.at[micro, pl.ds(me * CAP, CAP)],
+                    send_sem=leave_sem.at[chunk],
+                    recv_sem=came_sem.at[micro],
+                    device_id={"pipe": to_stage, "expert": place * GROUPS + group},
+                    device_id_type=MESH,
+                ).start()
             return carry
 
-        lax.fori_loop(0, homes, send, 0)
+        lax.fori_loop(0, zs, send, 0)
 
     def spread(chunk, land):
         flat[...] = land[chunk].astype(F32).reshape(rows * tiles, LANES)
@@ -196,7 +221,7 @@
         @pl.when(stage < last)
         def _():
             gather_rows(chunk, leave_f)
-            send_home(chunk, stage + 1, leave_f, sems.at[2], home_f_in, sems.at[0])
+            send_home(chunk, lax.rem(stage + 2, stages), leave_f, sems.at[2], home_f_in, sems.at[0])
 
     def backward(chunk):
         drain(land_b.at[chunk], sems.at[5].at[chunk])
@@ -246,48 +271,57 @@
                 centred = mixed[:, strip(at)] - scaled * mean
                 flat[tile_rows(at), :] = up_grad[:, strip(at)] + inverse * centred
             gather_rows(chunk, leave_b)
-            send_home(chunk, stage - 1, leave_b, sems.at[6], home_b_in, sems.at[4])
+            send_home(chunk, lax.rem(stage + stages - 2, stages), leave_b, sems.at[6], home_b_in, sems.at[4])
 
     is_last = stage == last
 
+    serve_f = jnp.where(stage == 0, 2 * chunks, 0)
+    serve_b = jnp.where(stage == last - 1, 0, jnp.where(is_last, 4 * chunks, 3 * chunks))
+    run_b = jnp.where(is_last, chunks, 4 * chunks)
+    next_f = lax.rem(stage + stages - 1, stages)
+    next_b = lax.rem(stage + 1, stages)
+
+    def within(at):
+        return (at >= 0) & (at < chunks)
+
+    def served(at):
+        return within(at) & (lax.rem(at + 4 * chunks, GROUPS) == my_group)
+
     def step(turn, carry):
-        @pl.when((turn < chunks) & (lax.rem(turn, GROUPS) == my_group))
+        @pl.when(served(turn - serve_b))
         def _():
             home(
-                turn, 0, stage == 0, home_f_in, sems.at[0],
+                turn - serve_b, 1, next_b, next_b == last, 0, home_b_in, sems.at[4],
+                home_b_out, sems.at[7], land_b, sems.at[5],
+            )
+
+        @pl.when(served(turn - serve_f))
+        def _():
+            home(
+                turn - serve_f, 0, next_f, next_f == 0, PACE, home_f_in, sems.at[0],
                 home_f_out, sems.at[3], land_f, sems.at[1],
             )
 
-        @pl.when(turn == 1)
+        @pl.when(turn == chunks)
         def _():
             load_in.wait()
             load_out.wait()
 
-        @pl.when((turn >= 1) & (turn <= chunks))
-        def _():
-            forward(turn - 1)
-
-        back = jnp.where(is_last, turn, turn - chunks)
-
-        @pl.when((back >= 0) & (back < chunks) & (lax.rem(back + chunks, GROUPS) == my_group))
-        def _():
-            home(
-                back, 1, is_last, home_b_in, sems.at[4],
-                home_b_out, sems.at[7], land_b, sems.at[5],
-            )
-
-        @pl.when((back >= 1) & (back <= chunks))
-        def _():
-            backward(back - 1)
+        @pl.when(within(turn - chunks))
+        def _():
+            forward(turn - chunks)
+
+        @pl.when(within(turn - run_b))
+        def _():
+            backward(turn - run_b)
 
         return carry
 
-    lax.fori_loop(0, 2 * chunks + 1, step, 0)
+    lax.fori_loop(0, 5 * chunks, step, 0)
 
     for micro in range(micros):
-        away = pl.ds(0, slots - CAP)
-        drain(home_f_out.at[micro, away], sems.at[3].at[micro])
-        drain(home_b_out.at[micro, away], sems.at[7].at[micro])
+        drain(home_f_out.at[micro], sems.at[3].at[micro])
+        drain(home_b_out.at[micro], sems.at[7].at[micro])
 
     @pl.when(stage < last)
     def _():
@@ -302,22 +336,26 @@
 
 def row_tables(routes, stage, stages, slots):
     ids = routes[..., 0]
-
-    def positions(layer):
-        own = lax.dynamic_index_in_dim(ids, layer, 0, keepdims=False)
-        order = jnp.arange(own.shape[1], dtype=jnp.int32)
-        before = order[:, None] > order[None, :]
-        same = (own[:, :, None] == own[:, None, :]) & before[None]
-        return own * CAP + jnp.sum(same.astype(jnp.int32), axis=2)
-
-    here = positions(stage)
-    token = jnp.broadcast_to(jnp.arange(here.shape[1], dtype=jnp.int32)[None], here.shape)
-    below = jnp.where(stage == 0, token, positions(jnp.maximum(stage - 1, 0)))
-    above = jnp.where(stage == stages - 1, token, positions(jnp.minimum(stage + 1, stages - 1)))
-    places = jnp.arange(slots, dtype=jnp.int32)
-    hit = here[:, :, None] == places[None, None, :]
-    pairs = jnp.stack([below, above])
-    table = slots + jnp.sum(jnp.where(hit[None], pairs[..., None] - slots, 0), axis=2)
+    order = jnp.arange(ids.shape[2], dtype=jnp.int32)
+    before = order[:, None] > order[None, :]
+    same = (ids[..., :, None] == ids[..., None, :]) & before
+    positions = ids * CAP + jnp.sum(same.astype(jnp.int32), axis=3)
+
+    def layer(index):
+        return lax.dynamic_index_in_dim(positions, jnp.clip(index, 0, stages - 1), 0, False)
+
+    to_f = lax.rem(stage + stages - 1, stages)
+    to_b = lax.rem(stage + 1, stages)
+    token = jnp.broadcast_to(order[None], ids.shape[1:])
+    here = jnp.stack([layer(to_f), layer(to_b)])
+    there = jnp.stack(
+        [
+            jnp.where(to_f == 0, token, layer(to_f - 1)),
+            jnp.where(to_b == stages - 1, token, layer(to_b + 1)),
+        ]
+    )
+    hit = here[..., None] == jnp.arange(slots, dtype=jnp.int32)
+    table = slots + jnp.sum(jnp.where(hit, there[..., None] - slots, 0), axis=2)
     return table.reshape(-1)
 
 
@@ -337,12 +375,11 @@
     slots = ranks * CAP
     chunks = micros * GROUPS
     rows = slots // GROUPS
-    source = jnp.where(stage == stages - 1, out_grad, tokens_in)
+    source = jnp.where(stage == stages - 2, out_grad, tokens_in)
     source = source.reshape(micros, tokens, tiles, LANES)
     tables = row_tables(routes, stage, stages, slots)
     chosen = (jnp.arange(ranks, dtype=jnp.int32) == me).astype(BF16)[None]
     column = lax.dot_general(chosen, router[0], NT, preferred_element_type=F32)
-    gain = norm_gain.astype(F32)
 
     vmem = pl.BlockSpec(memory_space=pltpu.VMEM)
     anywhere = pl.BlockSpec(memory_space=pl.ANY)
@@ -373,6 +410,7 @@
             pltpu.VMEM((chunks, rows, LANES), F32),
             pltpu.VMEM((rows, width), F32),
             pltpu.VMEM((rows, width), F32),
+            pltpu.VMEM((1, width), F32),
             pltpu.SemaphoreType.DMA((8, chunks)),
             pltpu.SemaphoreType.DMA((2,)),
         ],
@@ -380,7 +418,7 @@
             has_side_effects=True, vmem_limit_bytes=56 * 1024 * 1024
         ),
         name="relay",
-    )(tables, source, gain, column, w_in, w_out)
+    )(tables, source, norm_gain, column, w_in, w_out)
     normed, joined, activated, scaled = parts
     return (weight_grad(normed, joined), weight_grad(activated, scaled))
 

time: 415 us -> 372 us (0.90)
  Pallas kernels: 400 us -> 359 us
    pallas_call x1, Pallas kernels: 400 us -> 359 us  [shards(): pl.pallas_call(functools.partial(relay, stages, ranks, micros, tokens), o...]
where the time goes in v2:
time: 372 us
  Pallas kernels  359 us (97%)
  matrix products  7.42 us (2%)
    pallas_call x1, Pallas kernels, shards(): pl.pallas_call(functools.partial(relay, stages, ranks, micros, tokens), o...  359 us

profile of v2, /device:TPU:1, one launch (start us, length us, event | category | flops | bytes accessed | tf_op | source)
XLA Modules:
  0.0 371.7 jit_solution(10841495055372759942)
XLA Ops:
  0.6 0.0 copy-start
  0.7 1.3 convert_reduce_fusion
  2.0 0.7 multiply_add_fusion
  2.7 0.2 select_reduce_fusion
  2.9 0.7 add.40.tables
  3.6 1.2 broadcast_select_fusion
  4.7 1.0 copy.9
  5.7 0.0 copy-done
  5.7 0.7 fusion.2.column
  6.4 358.6 %relay.1 = (bf16[8,24,2048]{2,1,0:T(8,128)(2,1)}, bf16[8,24,1024]{2,1,0:T(8,128)(2,1)}, bf16[8,24,512]{2,1,0:T(8,128)(2,1)}, bf16[8,24,2048]{2,1,0:T(8,128)(2,1)}) custom-call(s32[384]{0:T(512)} %add.40.tables, bf16[2,80,16,128]{3,2,1,0:T(8,128)(2,1)} %bitcast.28, bf16[1,2048]{1,0:T(2,128)(2,1)} %gain_given.1, f32[1,2048]{1,0:T(1,128)} %fusion.2.column, ...), custom_call_target="tpu_custom_call" | custom-call | tf_op jit(solution)/shard_map/relay/pallas_call | solution.py:386
  365.0 0.0 copy-start.1
  365.0 0.0 copy-start.2
  365.0 4.6 %fusion = bf16[1,1,2048,1024]{3,2,1,0:T(8,128)(2,1)} fusion(bf16[8,24,2048]{2,1,0:T(8,128)(2,1)} %get-tuple-element.6, bf16[8,24,1024]{2,1,0:T(8,128)(2,1)} %get-tuple-element.7), kind=kOutput, calls=%fused_computation.2 | convolution fusion | flops 807403520 | bytes 5373952 | tf_op jit(solution)/shard_map/dot_general | solution.py:364
  369.7 0.0 copy-done.1
  369.7 0.0 copy-done.2
  369.7 2.1 fusion.1
  (4 shorter events, 0.0 us)
Async XLA Ops:
  0.6 5.1 %copy-start = (bf16[1,2048,32]{1,2,0:T(8,128)(2,1)S(1)}, bf16[1,2048,32]{1,2,0:T(8,128)(2,1)}, u32[]{:S(2)}) copy-start(bf16[1,2048,32]{1,2,0:T(8,128)(2,1)} %param.10) | copy-start | bytes 393220
  365.0 4.6 %copy-start.1 = (bf16[8,24,2048]{2,1,0:T(8,128)(2,1)S(1)}, bf16[8,24,2048]{2,1,0:T(8,128)(2,1)}, u32[]{:S(2)}) copy-start(bf16[8,24,2048]{2,1,0:T(8,128)(2,1)} %get-tuple-element.9) | copy-start | bytes 2359300
  365.0 4.6 %copy-start.2 = (bf16[8,24,512]{2,1,0:T(8,128)(2,1)S(1)}, bf16[8,24,512]{2,1,0:T(8,128)(2,1)}, u32[]{:S(2)}) copy-start(bf16[8,24,512]{2,1,0:T(8,128)(2,1)} %get-tuple-element.8) | copy-start | bytes 589828

commit v3 on v2

--- a/solution.py
+++ b/solution.py
@@ -10,7 +10,7 @@
 epsilon = 1e-06
 CAP = 3
 GROUPS = 4
-PACE = 8
+PACE = 12
 LANES = 128
 F32 = jnp.float32
 BF16 = jnp.bfloat16
@@ -112,13 +112,13 @@
         base = (table_row * micros + micro) * slots
 
         def place(step, carry):
-            for inside in range(CAP):
-                slot = step * CAP + inside
+            for inside in range(4 * CAP):
+                slot = step * (4 * CAP) + inside
                 out[micro, slot] = staging[tables[base + slot]]
             return carry
 
         def again(step, carry):
-            lax.fori_loop(0, ranks, place, 0)
+            lax.fori_loop(0, ranks // 4, place, 0)
             return carry
 
         lead = jnp.where(chunk < GROUPS, chunk, GROUPS)

time: 372 us -> 368 us (0.989)
  Pallas kernels: 359 us -> 355 us
where the time goes in v3:
time: 368 us
  Pallas kernels  355 us (96%)
  matrix products  7.42 us (2%)
    pallas_call x1, Pallas kernels, shards(): pl.pallas_call(functools.partial(relay, stages, ranks, micros, tokens), o...  355 us

profile of v3, /device:TPU:1, one launch (start us, length us, event | category | flops | bytes accessed | tf_op | source)
XLA Modules:
  0.0 368.2 jit_solution(14830232711513552574)
XLA Ops:
  0.6 0.0 copy-start
  0.7 1.3 convert_reduce_fusion
  2.0 0.7 multiply_add_fusion
  2.7 0.2 select_reduce_fusion
  2.9 0.7 add.40.tables
  3.6 1.2 broadcast_select_fusion
  4.7 1.0 copy.9
  5.7 0.0 copy-done
  5.7 0.7 fusion.2.column
  6.4 355.1 %relay.1 = (bf16[8,24,2048]{2,1,0:T(8,128)(2,1)}, bf16[8,24,1024]{2,1,0:T(8,128)(2,1)}, bf16[8,24,512]{2,1,0:T(8,128)(2,1)}, bf16[8,24,2048]{2,1,0:T(8,128)(2,1)}) custom-call(s32[384]{0:T(512)} %add.40.tables, bf16[2,80,16,128]{3,2,1,0:T(8,128)(2,1)} %bitcast.28, bf16[1,2048]{1,0:T(2,128)(2,1)} %gain_given.1, f32[1,2048]{1,0:T(1,128)} %fusion.2.column, ...), custom_call_target="tpu_custom_call" | custom-call | tf_op jit(solution)/shard_map/relay/pallas_call | solution.py:386
  361.5 0.0 copy-start.1
  361.5 0.0 copy-start.2
  361.5 4.6 %fusion = bf16[1,1,2048,1024]{3,2,1,0:T(8,128)(2,1)} fusion(bf16[8,24,2048]{2,1,0:T(8,128)(2,1)} %get-tuple-element.6, bf16[8,24,1024]{2,1,0:T(8,128)(2,1)} %get-tuple-element.7), kind=kOutput, calls=%fused_computation.2 | convolution fusion | flops 807403520 | bytes 5373952 | tf_op jit(solution)/shard_map/dot_general | solution.py:364
  366.1 0.0 copy-done.1
  366.2 0.0 copy-done.2
  366.2 2.1 fusion.1
  (4 shorter events, 0.0 us)
Async XLA Ops:
  0.6 5.1 %copy-start = (bf16[1,2048,32]{1,2,0:T(8,128)(2,1)S(1)}, bf16[1,2048,32]{1,2,0:T(8,128)(2,1)}, u32[]{:S(2)}) copy-start(bf16[1,2048,32]{1,2,0:T(8,128)(2,1)} %param.10) | copy-start | bytes 393220
  361.5 4.6 %copy-start.1 = (bf16[8,24,2048]{2,1,0:T(8,128)(2,1)S(1)}, bf16[8,24,2048]{2,1,0:T(8,128)(2,1)}, u32[]{:S(2)}) copy-start(bf16[8,24,2048]{2,1,0:T(8,128)(2,1)} %get-tuple-element.9) | copy-start | bytes 2359300
  361.5 4.6 %copy-start.2 = (bf16[8,24,512]{2,1,0:T(8,128)(2,1)S(1)}, bf16[8,24,512]{2,1,0:T(8,128)(2,1)}, u32[]{:S(2)}) copy-start(bf16[8,24,512]{2,1,0:T(8,128)(2,1)} %get-tuple-element.8) | copy-start | bytes 589828
